TPU v7x, 32 devices: a whole 2x2x4 slice. The times are simulated.
32 devices in a mesh: wide: 8 (over z, y), narrow: 4 (over x, core).
Axes of the slice: x: 2, y: 2, z: 4, core: 2. Of those that a mesh axis runs over, the one named last changes fastest.
Arguments:
- entry_factor: bfloat16 [288, 4, 64, 1024], P('wide', 'narrow'), may hold values from -6 to 6
- entry_panel: int32 [288, 4], P('wide', 'narrow'), may hold values from 0 to 1
- entry_target: int32 [288, 4], P('wide', 'narrow'), may hold values from 0 to 7, as said below
- entry_count: int32 [4, 8], P('narrow', 'wide'), may hold values from 1 to 36, 96 in all within a row
- panel_shared: bfloat16 [16, 64, 1024], P('wide', None, 'narrow'), may hold values from -0.1875 to 0.1875
- coupling: float32 [16, 64, 64], P('wide'), may hold values from -0.75 to 0.75
- probes: bfloat16 [32, 64, 1024], P('narrow'), may hold values from -6 to 6
Outputs:
- left_factor: float32 [32, 64, 1024], P('narrow', None, 'wide')
- right_factor: float32 [32, 64, 1024], P('narrow', None, 'wide')
Inputs may be any that keep to these rules, and one draw needn't show every extreme that they name: `entry_panel`: the local panel of an entry of any slot, live or not. `entry_target`: the local target of an entry; every target has at least one live entry. `entry_count`: the live slots of one device; for every owner the counts over the 8 wide indices sum to 96, and some device holds exactly 36.
All inputs are finite; a program needn't handle non-finite values.
Results may differ from a plain program's by a relative error of at most 0.0036.
Values may be sent and summed in bfloat16 or wider, within the bound.
A program may use at most 64 MiB of HBM per device.

v0:
```python
import math
import jax
import jax.numpy as jnp
from jax import lax
from jax.sharding import PartitionSpec as P


def shards(entry_factor, entry_panel, entry_target, entry_count, panel_shared, coupling, probes):
    highest = lax.Precision.HIGHEST
    factors = entry_factor[:, 0]
    slot_count = factors.shape[0]
    rank_dim = factors.shape[1]
    full_width = factors.shape[2]
    panel_count = panel_shared.shape[0]
    target_count = probes.shape[0]
    live_mask = (jnp.arange(slot_count) < entry_count[0, 0]).astype(jnp.float32)
    pick_panel = (entry_panel == jnp.arange(panel_count)[None, :]).astype(jnp.float32) * live_mask[
        :, None
    ]
    pick_target = (entry_target == jnp.arange(target_count)[None, :]).astype(jnp.float32)
    pair_pick = (pick_panel[:, :, None] * pick_target[:, None, :]).reshape(
        slot_count, panel_count * target_count
    )
    gathered = lax.all_gather(panel_shared, "narrow", axis=2, tiled=True)
    projected = jnp.einsum("drb,tkb->dtrk", gathered, probes, preferred_element_type=jnp.float32)
    coefficients = jnp.einsum("dij,dtjk->dtik", coupling, projected, precision=highest).astype(
        jnp.bfloat16
    )
    coeff_table = coefficients.reshape(panel_count * target_count, rank_dim * rank_dim)
    chosen = jnp.dot(
        pair_pick.astype(jnp.bfloat16), coeff_table, preferred_element_type=jnp.float32
    )
    chosen = chosen.astype(jnp.bfloat16).reshape(slot_count, rank_dim, rank_dim)
    contributions = jnp.einsum("eji,ejb->eib", chosen, factors, preferred_element_type=jnp.float32)
    sketch = jnp.einsum("et,eib->tib", pick_target, contributions, precision=highest)
    wide_count = lax.axis_size("wide")
    share_cols = full_width // wide_count
    sketch_sum = lax.psum(sketch, "wide")
    gram_matrix = jnp.einsum("tib,tjb->tij", sketch_sum, sketch_sum, precision=highest)
    lower_factor = jnp.linalg.cholesky(gram_matrix)
    basis = jax.scipy.linalg.solve_triangular(lower_factor, sketch_sum, lower=True)
    basis_round = basis.astype(jnp.bfloat16)
    own_basis = lax.dynamic_slice_in_dim(basis, lax.axis_index("wide") * share_cols, share_cols, 2)
    selected = jnp.einsum(
        "et,tkb->ekb",
        pick_target.astype(jnp.bfloat16),
        basis_round,
        preferred_element_type=jnp.float32,
    )
    selected = selected.astype(jnp.bfloat16)
    back_terms = jnp.einsum("eib,ekb->eik", factors, selected, preferred_element_type=jnp.float32)
    summed = jnp.einsum("ep,eik->pik", pair_pick, back_terms, precision=highest)
    summed = summed.reshape(panel_count, target_count, rank_dim, rank_dim)
    middle_terms = jnp.einsum("dtik,dij->dtkj", summed, coupling, precision=highest)
    partial_rows = jnp.einsum(
        "dtkj,djb->tkb", middle_terms, gathered.astype(jnp.float32), precision=highest
    )
    coeff_part = lax.psum_scatter(partial_rows, "wide", scatter_dimension=2, tiled=True)
    root_width = math.sqrt(full_width)
    return (own_basis * root_width, coeff_part / root_width)


def solution(mesh):
    placed = (
        P("wide", "narrow", None, None),
        P("wide", "narrow"),
        P("wide", "narrow"),
        P("narrow", "wide"),
        P("wide", None, "narrow"),
        P("wide", None, None),
        P("narrow", None, None),
    )
    return jax.shard_map(
        shards,
        mesh=mesh,
        in_specs=placed,
        out_specs=(P("narrow", None, "wide"), P("narrow", None, "wide")),
        check_vma=False,
    )
```

profile of v0, /device:TPU:0, one launch (start us, length us, event | category | flops | bytes accessed | tf_op | source)
XLA Modules:
  0.0 328.4 jit_solution(10725598671400621314)
XLA Ops:
  7.2 0.0 copy-start
  7.2 0.0 copy-start.4
  7.2 0.0 copy-start.6
  7.2 0.0 all-reduce.2.cloned.1.call-start
  7.2 0.7 fusion.36
  8.0 7.4 %all_gather.3 = bf16[2,64,1024]{2,1,0:T(8,128)(2,1)S(1)} all-gather(bf16[2,64,256]{2,1,0:T(8,128)(2,1)} %param.11), channel_id=1, replica_groups=mesh['wide'=8,'narrow'=4] {'narrow'}, dimensions={2}, use_global_device_ids=true | all-gather | bytes 327680 | tf_op jit(solution)/shard_map/all_gather | solution.py:24
  15.4 0.0 copy-done
  15.4 0.0 copy-start.2
  15.4 0.5 convolution_bitcast_fusion.1
  15.9 0.2 copy-done.2
  16.1 0.0 copy-done.4
  16.1 0.6 fusion.18
  16.7 0.2 copy.21
  16.9 0.3 reshape.98
  17.8 0.0 copy-done.6
  17.9 0.3 convolution_convert_fusion
  18.1 0.6 reshape.99
  18.8 0.0 copy-start.5
  18.8 3.8 %fusion.4 = f32[36,64,1024]{2,1,0:T(8,128)S(1)} fusion(bf16[36,64,64]{2,1,0:T(8,128)(2,1)S(1)} %reshape.99, bf16[36,1,64,1024]{3,2,1,0:T(8,128)(2,1)} %param.7), kind=kOutput, calls=%fused_computation.4 | convolution fusion | flops 301989888 | bytes 14450688 | tf_op jit(solution)/shard_map/eji,ejb->eib/dot_general | solution.py:34
  22.6 0.0 copy-done.5
  22.6 10.1 %fusion = f32[8,64,1024]{2,0,1:T(8,128)} fusion(f32[36,64,1024]{2,1,0:T(8,128)S(1)} %fusion.4, s32[36]{0:T(128)S(1)} %bitcast.78), kind=kOutput, calls=%fused_computation | convolution fusion | flops 226492704 | bytes 11534480 | tf_op jit(solution)/shard_map/et,eib->tib/dot_general | solution.py:35
  32.7 0.0 all-reduce.2.cloned.1.call-update
  32.7 0.0 reduce-scatter.2.cloned.1.call-start
  32.8 103.7 %all-reduce.2.cloned.1.call-done = f32[8,64,1024]{2,0,1:T(8,128)} async-done(((f32[8,64,1024]{2,0,1:T(8,128)}), f32[8,64,1024]{2,0,1:T(8,128)}) %all-reduce.2.cloned.1.call-update) | async-done | bytes 2097168 | tf_op jit(solution)/shard_map/psum | solution.py:38
  136.4 0.0 copy-start.1
  136.4 6.7 %fusion.9 = f32[8,64,64]{2,1,0:T(8,128)S(1)} fusion(f32[8,64,1024]{2,0,1:T(8,128)} %all-reduce.2.cloned.1.call-done), kind=kOutput, calls=%fused_computation.11 | convolution fusion | flops 402653184 | bytes 2228224 | tf_op jit(solution)/shard_map/tib,tjb->tij/dot_general | solution.py:39
  143.1 0.8 copy.26
  144.0 1.7 fusion.25
  145.7 47.6 %custom-call.8 = f32[8,64,64]{2,1,0:T(8,128)S(1)} custom-call(f32[8,64,64]{2,1,0:T(8,128)} %fusion.25), custom_call_target="Cholesky" | custom-call | tf_op jit(solution)/shard_map/jit(cholesky)/cholesky | solution.py:40
  193.3 0.1 compare_reduce_fusion
  193.4 0.8 select_bitcast_fusion
  194.3 40.3 %custom-call.9 = f32[8,1,64,64]{2,3,1,0:T(8,128)S(1)} custom-call(f32[8,1,64,64]{3,2,1,0:T(8,128)} %select_bitcast_fusion), custom_call_target="InvertDiagBlocksLowerTriangular" | custom-call | tf_op jit(solution)/shard_map/jit(_solve_triangular)/vmap()/triangular_solve | solution.py:41
  234.5 0.0 copy-done.1
  234.5 4.4 %fusion.42 = (bf16[8,64,1024]{2,1,0:T(8,128)(2,1)S(1)}, f32[8,64,1024]{2,1,0:T(8,128)}) fusion(f32[8,64,1024]{2,0,1:T(8,128)S(1)} %copy-done.1, f32[8,1,64,64]{2,3,1,0:T(8,128)S(1)} %custom-call.9), kind=kOutput, calls=%fused_computation.53 | convolution fusion | flops 403177472 | bytes 5373952 | tf_op jit(solution)/shard_map/jit(_solve_triangular)/vmap()/triangular_solve | solution.py:41
  238.9 1.6 convolution_convert_fusion.1
  240.5 5.5 %fusion.11 = f32[36,64,64]{1,2,0:T(8,128)S(1)} fusion(bf16[36,1,64,1024]{3,2,1,0:T(8,128)(2,1)} %param.7, bf16[36,64,1024]{2,0,1:T(8,128)(2,1)S(1)} %convolution_convert_fusion.1), kind=kOutput, calls=%fused_computation.14 | convolution fusion | flops 301989888 | bytes 10027008 | tf_op jit(solution)/shard_map/eib,ekb->eik/dot_general | solution.py:51
  246.0 0.5 copy.31
  246.5 0.0 copy-start.3
  246.5 0.8 fusion.16
  247.3 1.8 fusion.21
  249.1 0.0 copy-done.3
  249.1 2.3 convolution_bitcast_fusion
  251.4 0.0 reduce-scatter.2.cloned.1.call-update
  251.5 1.7 dynamic-slice_multiply_fusion
  253.1 66.7 %reduce-scatter.2.cloned.1.call-done = f32[8,64,128]{2,1,0:T(8,128)} async-done(((f32[8,64,1024]{2,1,0:T(8,128)}), f32[8,64,128]{2,1,0:T(8,128)}) %reduce-scatter.2.cloned.1.call-update) | async-done | bytes 262160 | tf_op jit(solution)/shard_map/reduce_scatter | solution.py:58
  319.8 1.7 broadcast_multiply_fusion
  (5 shorter events, 0.1 us)
Async XLA Ops:
  7.2 8.2 %copy-start = (bf16[8,64,1024]{2,1,0:T(8,128)(2,1)S(1)}, bf16[8,64,1024]{2,1,0:T(8,128)(2,1)}, u32[]{:S(2)}) copy-start(bf16[8,64,1024]{2,1,0:T(8,128)(2,1)} %param.13) | copy-start | bytes 3145732
  7.2 8.9 %copy-start.4 = (f32[2,64,64]{2,1,0:T(8,128)S(1)}, f32[2,64,64]{2,1,0:T(8,128)}, u32[]{:S(2)}) copy-start(f32[2,64,64]{2,1,0:T(8,128)} %param.12) | copy-start | bytes 98308
  7.2 10.6 %copy-start.6 = (s32[36,1]{0,1:T(1,128)S(1)}, s32[36,1]{0,1:T(1,128)}, u32[]{:S(2)}) copy-start(s32[36,1]{0,1:T(1,128)} %param.8) | copy-start | bytes 436
  7.2 129.2 %all-reduce.2.cloned.1.call-start = ((), (), s32[]{:S(2)}) async-start(), calls=%async_computation.1 | async-start | bytes 4194304 | tf_op jit(solution)/shard_map/psum | solution.py:38
  15.4 0.7 copy-start.2
  18.8 3.8 %copy-start.5 = (s32[36,1]{0,1:T(1,128)S(1)}, s32[36,1]{0,1:T(1,128)}, u32[]{:S(2)}) copy-start(s32[36,1]{0,1:T(1,128)} %param.9) | copy-start | bytes 436
  32.7 287.2 %reduce-scatter.2.cloned.1.call-start = ((), (), s32[]{:S(2)}) async-start(), calls=%async_computation.2 | async-start | bytes 2359296 | tf_op jit(solution)/shard_map/reduce_scatter | solution.py:58
  136.4 98.1 %copy-start.1 = (f32[8,64,1024]{2,0,1:T(8,128)S(1)}, f32[8,64,1024]{2,0,1:T(8,128)}, u32[]{:S(2)}) copy-start(f32[8,64,1024]{2,0,1:T(8,128)} %all-reduce.2.cloned.1.call-done) | copy-start | bytes 6291460
  246.5 2.6 copy-start.3
Sparse Core Ops, SparseCore 0:
  32.8 103.5 all-reduce.1
  251.6 68.2 reduce-scatter.1
where the time goes:
time: 329 us; the launch traced here: 328 us
  waiting for transfers between devices  170 us (52%)
  other arithmetic  94.6 us (29%)
  matrix products  38.3 us (12%)
  between operations  14.9 us (5%)
  blocking collectives  7.42 us (2%)
    psum x1, waiting for transfers between devices, shards(): sketch_sum = lax.psum(sketch, 'wide')  104 us
    reduce_scatter x1, waiting for transfers between devices, shards(): lax.psum_scatter(partial_rows, 'wide', scatter_dimension=2, tiled=True)  66.7 us
    another operation x4, other arithmetic, shards(): lower_factor = jnp.linalg.cholesky(gram_matrix)  47.8 us
    another operation x3, other arithmetic, shards(): jax.scipy.linalg.solve_triangular(lower_factor, sketch_sum, lower=True)  41.1 us
    dot_general x1, matrix products, shards(): jnp.einsum('et,eib->tib', pick_target, contributions, precision=highest)  10.1 us
    all_gather x1, blocking collectives, shards(): gathered = lax.all_gather(panel_shared, 'narrow', axis=2, tiled=True)  7.42 us
    dot_general x1, matrix products, shards(): jnp.einsum('tib,tjb->tij', sketch_sum, sketch_sum, precision=highest)  6.7 us
  transfers between devices with their start and end apart: 2, of which 2 were waited for; matrix products, arithmetic and copies ran while one was open for 1% of the time, Pallas kernels for 0%

commit v1 on v0

--- a/solution.py
+++ b/solution.py
@@ -35,7 +35,11 @@
     sketch = jnp.einsum("et,eib->tib", pick_target, contributions, precision=highest)
     wide_count = lax.axis_size("wide")
     share_cols = full_width // wide_count
-    sketch_sum = lax.psum(sketch, "wide")
+    sketch_sum = sketch
+    for hop in (1, 2, 4):
+        sketch_sum = sketch_sum + lax.ppermute(
+            sketch_sum, "wide", [(dev, dev ^ hop) for dev in range(8)]
+        )
     gram_matrix = jnp.einsum("tib,tjb->tij", sketch_sum, sketch_sum, precision=highest)
     lower_factor = jnp.linalg.cholesky(gram_matrix)
     basis = jax.scipy.linalg.solve_triangular(lower_factor, sketch_sum, lower=True)

time: 329 us -> 412 us (1.25)
  waiting for transfers between devices: 170 us -> 250 us
  starting transfers between devices: 0.08 us -> 6.01 us
    ppermute x0 -> x3, waiting for transfers between devices: none -> 181 us  [shards(): lax.ppermute(sketch_sum, 'wide', [(dev, dev ^ hop) for dev in range(8)])]
    psum x1 -> x0, waiting for transfers between devices: 104 us -> none  [shards(): sketch_sum = lax.psum(sketch, 'wide')]
    ppermute x0 -> x3, starting transfers between devices: none -> 5.97 us  [shards(): lax.ppermute(sketch_sum, 'wide', [(dev, dev ^ hop) for dev in range(8)])]
  transfers between devices with their start and end apart: 2 -> 4, of which waited for: 2 -> 4; matrix products, arithmetic and copies ran while one was open for 1% -> 0% of each run, Pallas kernels for 0% -> 0%
where the time goes in v1:
time: 412 us
  waiting for transfers between devices  250 us (61%)
  other arithmetic  96 us (23%)
  matrix products  34.7 us (8%)
  between operations  14.9 us (4%)
  blocking collectives  7.42 us (2%)
  starting transfers between devices  6.01 us (1%)
    ppermute x3, waiting for transfers between devices, shards(): lax.ppermute(sketch_sum, 'wide', [(dev, dev ^ hop) for dev in range(8)])  181 us
    reduce_scatter x1, waiting for transfers between devices, shards(): lax.psum_scatter(partial_rows, 'wide', scatter_dimension=2, tiled=True)  68.9 us
    another operation x4, other arithmetic, shards(): lower_factor = jnp.linalg.cholesky(gram_matrix)  47.8 us
    another operation x3, other arithmetic, shards(): jax.scipy.linalg.solve_triangular(lower_factor, sketch_sum, lower=True)  41.1 us
    dot_general x1, matrix products, shards(): jnp.einsum('et,eib->tib', pick_target, contributions, precision=highest)  8.9 us
  transfers between devices with their start and end apart: 4, of which 4 were waited for; matrix products, arithmetic and copies ran while one was open for 0% of the time, Pallas kernels for 0%

profile of v1, /device:TPU:0, one launch (start us, length us, event | category | flops | bytes accessed | tf_op | source)
XLA Modules:
  0.0 411.7 jit_solution(8059848365727552496)
XLA Ops:
  7.2 0.0 copy-start
  7.2 0.0 copy-start.3
  7.2 0.0 copy-start.5
  7.2 0.0 reduce-scatter.2.cloned.1.call-start
  7.2 0.7 fusion.36
  8.0 7.4 %all_gather.3 = bf16[2,64,1024]{2,1,0:T(8,128)(2,1)S(1)} all-gather(bf16[2,64,256]{2,1,0:T(8,128)(2,1)} %param.11), channel_id=1, replica_groups=mesh['wide'=8,'narrow'=4] {'narrow'}, dimensions={2}, use_global_device_ids=true | all-gather | bytes 327680 | tf_op jit(solution)/shard_map/all_gather | solution.py:24
  15.4 0.0 copy-done
  15.4 0.5 convolution_bitcast_fusion.1
  15.9 0.2 copy-done.1
  16.1 0.0 copy-done.3
  16.1 0.6 fusion.18
  16.7 0.2 copy.21
  16.9 0.3 reshape.98
  17.8 0.0 copy-done.5
  17.9 0.3 convolution_convert_fusion
  18.1 0.6 reshape.99
  18.8 0.0 copy-start.4
  18.8 3.8 fusion.4
  22.6 0.0 copy-done.4
  22.6 8.9 %fusion = f32[8,64,1024]{2,0,1:T(8,128)S(1)} fusion(f32[36,64,1024]{2,1,0:T(8,128)S(1)} %fusion.4, s32[36]{0:T(128)S(1)} %bitcast.78), kind=kOutput, calls=%fused_computation | convolution fusion | flops 226492704 | bytes 11534480 | tf_op jit(solution)/shard_map/et,eib->tib/dot_general | solution.py:35
  31.5 1.6 collective-permute-start
  33.1 46.3 %collective-permute-done = f32[8,64,1024]{2,0,1:T(8,128)S(1)} collective-permute-done((f32[8,64,1024]{2,0,1:T(8,128)S(1)}, f32[8,64,1024]{2,0,1:T(8,128)S(1)}, u32[]{:S(2)}, u32[]{:S(2)}) %collective-permute-start) | collective-permute-done | bytes 2097184 | tf_op jit(solution)/shard_map/ppermute | solution.py:40
  79.4 0.4 add.26
  79.8 1.7 collective-permute-start.1
  81.5 45.4 %collective-permute-done.1 = f32[8,64,1024]{2,0,1:T(8,128)S(1)} collective-permute-done((f32[8,64,1024]{2,0,1:T(8,128)S(1)}, f32[8,64,1024]{2,0,1:T(8,128)S(1)}, u32[]{:S(2)}, u32[]{:S(2)}) %collective-permute-start.1) | collective-permute-done | bytes 2097184 | tf_op jit(solution)/shard_map/ppermute | solution.py:40
  126.9 0.6 add.27
  127.5 2.7 collective-permute-start.2
  130.2 89.4 %collective-permute-done.2 = f32[8,64,1024]{2,0,1:T(8,128)S(1)} collective-permute-done((f32[8,64,1024]{2,0,1:T(8,128)S(1)}, f32[8,64,1024]{2,0,1:T(8,128)S(1)}, u32[]{:S(2)}, u32[]{:S(2)}) %collective-permute-start.2) | collective-permute-done | bytes 2097184 | tf_op jit(solution)/shard_map/ppermute | solution.py:40
  219.5 0.4 add.28
  219.9 4.4 %fusion.9 = f32[8,64,64]{2,1,0:T(8,128)S(1)} fusion(f32[8,64,1024]{2,0,1:T(8,128)S(1)} %add.28), kind=kOutput, calls=%fused_computation.11 | convolution fusion | flops 402653184 | bytes 2228224 | tf_op jit(solution)/shard_map/tib,tjb->tij/dot_general | solution.py:43
  224.3 0.8 copy.26
  225.1 1.7 fusion.25
  226.8 47.6 %custom-call.8 = f32[8,64,64]{2,1,0:T(8,128)S(1)} custom-call(f32[8,64,64]{2,1,0:T(8,128)} %fusion.25), custom_call_target="Cholesky" | custom-call | tf_op jit(solution)/shard_map/jit(cholesky)/cholesky | solution.py:44
  274.5 0.1 compare_reduce_fusion
  274.6 0.8 select_bitcast_fusion
  275.4 40.3 %custom-call.9 = f32[8,1,64,64]{2,3,1,0:T(8,128)S(1)} custom-call(f32[8,1,64,64]{3,2,1,0:T(8,128)} %select_bitcast_fusion), custom_call_target="InvertDiagBlocksLowerTriangular" | custom-call | tf_op jit(solution)/shard_map/jit(_solve_triangular)/vmap()/triangular_solve | solution.py:45
  315.7 4.4 %fusion.42 = (bf16[8,64,1024]{2,1,0:T(8,128)(2,1)S(1)}, f32[8,64,1024]{2,1,0:T(8,128)}) fusion(f32[8,64,1024]{2,0,1:T(8,128)S(1)} %add.28, f32[8,1,64,64]{2,3,1,0:T(8,128)S(1)} %custom-call.9), kind=kOutput, calls=%fused_computation.53 | convolution fusion | flops 403177472 | bytes 5373952 | tf_op jit(solution)/shard_map/jit(_solve_triangular)/vmap()/triangular_solve | solution.py:45
  320.1 1.6 convolution_convert_fusion.1
  321.7 5.5 %fusion.11 = f32[36,64,64]{1,2,0:T(8,128)S(1)} fusion(bf16[36,1,64,1024]{3,2,1,0:T(8,128)(2,1)} %param.7, bf16[36,64,1024]{2,0,1:T(8,128)(2,1)S(1)} %convolution_convert_fusion.1), kind=kOutput, calls=%fused_computation.14 | convolution fusion | flops 301989888 | bytes 10027008 | tf_op jit(solution)/shard_map/eib,ekb->eik/dot_general | solution.py:55
  327.1 0.5 copy.31
  327.6 0.0 copy-start.2
  327.6 0.8 fusion.16
  328.4 1.8 fusion.21
  330.2 2.3 convolution_bitcast_fusion
  332.6 0.0 reduce-scatter.2.cloned.1.call-update
  332.6 1.7 dynamic-slice_multiply_fusion
  334.3 68.9 %reduce-scatter.2.cloned.1.call-done = f32[8,64,128]{2,1,0:T(8,128)} async-done(((f32[8,64,1024]{2,1,0:T(8,128)}), f32[8,64,128]{2,1,0:T(8,128)}) %reduce-scatter.2.cloned.1.call-update) | async-done | bytes 262160 | tf_op jit(solution)/shard_map/reduce_scatter | solution.py:62
  403.1 1.7 broadcast_multiply_fusion
  (7 shorter events, 0.1 us)
Async XLA Ops:
  7.2 8.2 %copy-start = (bf16[8,64,1024]{2,1,0:T(8,128)(2,1)S(1)}, bf16[8,64,1024]{2,1,0:T(8,128)(2,1)}, u32[]{:S(2)}) copy-start(bf16[8,64,1024]{2,1,0:T(8,128)(2,1)} %param.13) | copy-start | bytes 3145732
  7.2 8.9 %copy-start.3 = (f32[2,64,64]{2,1,0:T(8,128)S(1)}, f32[2,64,64]{2,1,0:T(8,128)}, u32[]{:S(2)}) copy-start(f32[2,64,64]{2,1,0:T(8,128)} %param.12) | copy-start | bytes 98308
  7.2 10.6 %copy-start.5 = (s32[36,1]{0,1:T(1,128)S(1)}, s32[36,1]{0,1:T(1,128)}, u32[]{:S(2)}) copy-start(s32[36,1]{0,1:T(1,128)} %param.8) | copy-start | bytes 436
  7.2 395.9 %reduce-scatter.2.cloned.1.call-start = ((), (), s32[]{:S(2)}) async-start(), calls=%async_computation.1 | async-start | bytes 2359296 | tf_op jit(solution)/shard_map/reduce_scatter | solution.py:62
  15.4 0.7 copy-start.1
  18.8 3.8 copy-start.4
  31.5 47.9 %collective-permute-start = (f32[8,64,1024]{2,0,1:T(8,128)S(1)}, f32[8,64,1024]{2,0,1:T(8,128)S(1)}, u32[]{:S(2)}, u32[]{:S(2)}) collective-permute-start(f32[8,64,1024]{2,0,1:T(8,128)S(1)} %fusion), channel_id=1, source_target_pairs={{0,4},{4,0},{8,12},{12,8},{16,20},{20,16},{24,28},{28,24},{1,5},{5... | collective-permute-start | bytes 6291464 | tf_op jit(solution)/shard_map/ppermute | solution.py:40
  79.8 47.1 %collective-permute-start.1 = (f32[8,64,1024]{2,0,1:T(8,128)S(1)}, f32[8,64,1024]{2,0,1:T(8,128)S(1)}, u32[]{:S(2)}, u32[]{:S(2)}) collective-permute-start(f32[8,64,1024]{2,0,1:T(8,128)S(1)} %add.26), channel_id=1, source_target_pairs={{0,8},{4,12},{8,0},{12,4},{16,24},{20,28},{24,16},{28,20},{1,9},{5... | collective-permute-start | bytes 6291464 | tf_op jit(solution)/shard_map/ppermute | solution.py:40
  127.5 92.1 %collective-permute-start.2 = (f32[8,64,1024]{2,0,1:T(8,128)S(1)}, f32[8,64,1024]{2,0,1:T(8,128)S(1)}, u32[]{:S(2)}, u32[]{:S(2)}) collective-permute-start(f32[8,64,1024]{2,0,1:T(8,128)S(1)} %add.27), channel_id=1, source_target_pairs={{0,16},{4,20},{8,24},{12,28},{16,0},{20,4},{24,8},{28,12},{1,17},{... | collective-permute-start | bytes 6291464 | tf_op jit(solution)/shard_map/ppermute | solution.py:40
  327.6 2.6 copy-start.2
Sparse Core Ops, SparseCore 0:
  332.7 70.3 reduce-scatter.1
